TPU v7x, 256 devices: a whole 4x4x8 slice. The times are simulated.
256 devices in a mesh: rep: 16 (over y_lo, z), tp: 16 (over x, y_hi, core).
Axes of the slice: x: 4, y: 4 (y_hi: 2, y_lo: 2; y = y_hi * 2 + y_lo), z: 8, core: 2. Of those that a mesh axis runs over, the one named last changes fastest.
Arguments:
- tokens: bfloat16 [16384, 8192], P('rep', 'tp'), may hold values from -6 to 6
- grad_out: bfloat16 [16384, 4096], P('rep', 'tp'), may hold values from -0.046875 to 0.046875
- lengths: int32 [16, 16], replicated, may hold values from 0 to 256, as said below
- master: float32 [8192, 2048], P('rep', 'tp'), may hold values from -3 to 3
- first: float32 [8192, 2048], P('rep', 'tp'), may hold values from -6 to 6
- second: float32 [8192, 2048], P('rep', 'tp'), may hold values from 0.25 to 4
Outputs:
- new_master: float32 [8192, 2048], P('rep', 'tp')
- new_first: float32 [8192, 2048], P('rep', 'tp')
- new_second: float32 [8192, 2048], P('rep', 'tp')
- healthy_weights: bfloat16 [8192, 2048], P(None, 'tp')
- slot_weights: bfloat16 [16, 8192, 4096], P('rep', None, 'tp')
Inputs may be any that keep to these rules, and one draw needn't show every extreme that they name: `lengths`: each row is one replica's split of the 2048 columns over its devices in tp order: the entries are multiples of 64, sum to 2048, the nonzero ones come first and number at least half of the row; a row is either all 128 or has an entry equal to 256, and some row has an entry equal to 256.
All inputs are finite; a program needn't handle non-finite values.
Results may differ from a plain program's by a relative error of at most 0.0019.
Values may be sent and summed in bfloat16 or wider, within the bound.
No kernel may reach another device: no remote copies, remote signals or barrier semaphores. Data moves between devices by JAX's collectives and lax.ppermute only.
A program may use at most 128 MiB of HBM per device.

v0:
```python
import jax
import jax.numpy as jnp
from jax import lax
from jax.sharding import Mesh
from jax.sharding import PartitionSpec as P

COLS = 2048
STEP = 1000
REP = ("rep_0", "rep_1")
decay_first = 0.9
decay_second = 0.999
learning_rate = 0.02
weight_decay = 0.1
epsilon = 1e-08


def own_block(parts, axes, turns):
    inside = parts.shape[1:]
    parts = parts.reshape(*(lax.axis_size(a) for a in axes), *inside)
    parts = jnp.moveaxis(parts, turns, range(len(axes))).reshape(-1, *inside)
    for k in turns:
        parts = lax.psum_scatter(parts, axes[k], scatter_dimension=0, tiled=True)
    return parts[0]


def in_blocks(value, dim, size):
    before, after = (value.shape[:dim], value.shape[dim + 1 :])
    return jnp.moveaxis(value.reshape(*before, size, -1, *after), dim, 0)


def summed_rows(value, axes, turns, dim):
    size = lax.axis_size(axes)
    return own_block(in_blocks(value, dim, size), axes, turns)


def from_everyone(value, axis):
    copies = jnp.broadcast_to(value, (lax.axis_size(axis), *value.shape))
    return lax.all_to_all(copies, axis, split_axis=0, concat_axis=0, tiled=True)


def laid_out(parts, dim):
    shape = list(parts.shape[1:])
    shape[dim] *= parts.shape[0]
    return jnp.moveaxis(parts, 0, dim).reshape(shape)


def gathered_copies(value, axis, dim):
    parts = from_everyone(value, axis)
    return laid_out(parts, dim)


def adam_update(master, first, second, gradient):
    scale_first = 1.0 - decay_first**STEP
    scale_second = 1.0 - decay_second**STEP
    new_first = decay_first * first + (1.0 - decay_first) * gradient
    new_second = decay_second * second + (1.0 - decay_second) * gradient * gradient
    direction = new_first / scale_first / (jnp.sqrt(new_second / scale_second) + epsilon)
    new_master = master - learning_rate * (direction + weight_decay * master)
    return (new_master, new_first, new_second)


def on_device(tokens, grad_out, lengths, master, first, second):
    shards = lax.axis_size("tp")
    replicas = lax.axis_size(REP)
    column_index = lax.axis_index("tp")
    replica_index = lax.axis_index(REP)
    token_count = tokens.shape[0]
    slot_width = grad_out.shape[1]
    block_width = COLS // shards
    begins_all = jnp.cumsum(lengths, axis=1) - lengths
    is_mine = jnp.arange(shards, dtype=jnp.int32) == column_index
    own_lengths = lax.dynamic_index_in_dim(lengths, replica_index, 0, keepdims=False)
    own_begins = lax.dynamic_index_in_dim(begins_all, replica_index, 0, keepdims=False)
    my_begin = jnp.sum(jnp.where(is_mine, own_begins, 0))
    my_length = jnp.sum(jnp.where(is_mine, own_lengths, 0))
    columns = jnp.arange(COLS, dtype=jnp.int32)
    offset = columns - my_begin
    inside = (offset >= 0) & (offset < my_length)
    picked = jnp.take(grad_out, jnp.clip(offset, 0, slot_width - 1), axis=1)
    spread = jnp.where(inside[None, :], picked, jnp.zeros_like(picked)).reshape(
        token_count, shards, block_width
    )
    received = lax.all_to_all(spread, "tp", split_axis=1, concat_axis=1, tiled=True)
    grad_block = jnp.sum(received, axis=1)
    grad_columns = lax.dot_general(
        lax.all_gather(tokens, "tp", axis=1, tiled=True),
        grad_block,
        (((0,), (0,)), ((), ())),
        preferred_element_type=jnp.float32,
    )
    summed = summed_rows(grad_columns.astype(jnp.bfloat16), REP, (1, 0), 0).astype(jnp.float32)
    new_master, new_first, new_second = adam_update(master, first, second, summed)
    weights = new_master.astype(jnp.bfloat16)
    healthy = gathered_copies(weights, REP, 0)
    replica_rows = lax.all_gather(weights, "tp", axis=1, tiled=True)
    slot_begins = jnp.sum(jnp.where(is_mine[None, :], begins_all, 0), axis=1)
    slot_lengths = jnp.sum(jnp.where(is_mine[None, :], lengths, 0), axis=1)
    within = jnp.arange(slot_width, dtype=jnp.int32)
    source_cols = slot_begins[:, None] + within[None, :]
    valid = within[None, :] < slot_lengths[:, None]
    taken = jnp.take(replica_rows, jnp.clip(source_cols, 0, COLS - 1).reshape(-1), axis=1)
    outgoing = jnp.where(valid.reshape(-1)[None, :], taken, jnp.zeros_like(taken))
    outgoing = outgoing.reshape(replica_rows.shape[0], replicas, slot_width)
    arrived = lax.all_to_all(outgoing, REP, split_axis=1, concat_axis=0, tiled=True)
    slot_weights = arrived.reshape(1, -1, slot_width)
    return (new_master, new_first, new_second, healthy, slot_weights)


def solution(mesh):
    torus = Mesh(mesh.devices.reshape(2, 8, mesh.shape["tp"]), ("rep_0", "rep_1", "tp"))
    placed = (P(REP, "tp"), P(REP, "tp"), P(), P(REP, "tp"), P(REP, "tp"), P(REP, "tp"))
    return jax.shard_map(
        on_device,
        mesh=torus,
        in_specs=placed,
        out_specs=(P(REP, "tp"), P(REP, "tp"), P(REP, "tp"), P(None, "tp"), P(REP, None, "tp")),
        check_vma=False,
    )
```

profile of v0, /device:TPU:32, one launch (start us, length us, event | category | flops | bytes accessed | tf_op | source)
XLA Modules:
  0.0 450.8 jit_solution(10688095374911271748)
XLA Ops:
  7.2 0.0 all-gather.3.cloned.1.call-start
  7.2 0.7 all-gather.3.cloned.1.call-update
  7.9 0.0 reduce-scatter.3.cloned.1.call-start
  8.0 0.9 reduce_window_sum.11
  8.8 1.2 copy.34
  10.1 0.8 select_reduce_fusion.1
  10.9 1.3 fusion.12
  12.2 0.7 compare_select_fusion.1
  12.9 9.6 %gather_fusion = bf16[2048,1024]{1,0:T(8,128)(2,1)} fusion(bf16[1024,256]{0,1:T(8,128)(2,1)S(1)} %copy.34, s32[2048]{0:T(1024)S(1)} %broadcast_clamp_fusion.1), kind=kCustom, calls=%fused_computation | custom fusion | bytes 8396800 | tf_op jit(solution)/shard_map/jit(_take)/gather | solution.py:79
  22.5 0.7 fusion.10
  23.2 1.3 fusion.11
  24.5 3.1 select_select_fusion.1
  27.6 73.9 %all_to_all.25 = bf16[1024,16,128]{0,2,1:T(8,128)(2,1)} all-to-all(bf16[1024,16,128]{0,2,1:T(8,128)(2,1)S(1)} %select_select_fusion.1), channel_id=1, replica_groups=mesh['rep_0'=2,'rep_1'=8,'tp'=16] {'tp'}, dimensions={1} | all-to-all | bytes 8388608 | tf_op jit(solution)/shard_map/all_to_all | solution.py:83
  101.5 3.1 reduce_sum.50
  104.7 63.9 %all-gather.3.cloned.1.call-done = bf16[1024,8192]{1,0:T(8,128)(2,1)} async-done(((bf16[1024,512]{1,0:T(8,128)(2,1)}), bf16[1024,8192]{1,0:T(8,128)(2,1)}) %all-gather.3.cloned.1.call-update) | async-done | bytes 16777232 | tf_op jit(solution)/shard_map/all_gather | solution.py:86
  168.6 8.1 %convolution_convert_fusion = bf16[128,8192]{1,0:T(8,128)(2,1)S(1)} fusion(bf16[1024,128]{0,1:T(8,128)(2,1)S(1)} %reduce_sum.50, bf16[1024,8192]{1,0:T(8,128)(2,1)} %all-gather.3.cloned.1.call-done), kind=kOutput, calls=%fused_computation.2 | convolution fusion | flops 2148532224 | bytes 19136512 | tf_op jit(solution)/shard_map/dot_general | solution.py:85
  176.7 0.9 copy.44
  177.6 0.0 copy-start
  177.6 0.0 copy-start.1
  177.6 0.0 copy-start.2
  177.6 2.5 copy.35
  180.1 0.0 reduce-scatter.3.cloned.1.call-update
  180.1 0.0 reduce-scatter.5.cloned.1.call-start
  180.2 41.0 %reduce-scatter.3.cloned.1.call-done = bf16[2,512,128]{1,2,0:T(8,128)(2,1)} async-done(((bf16[16,512,128]{1,2,0:T(8,128)(2,1)}), bf16[2,512,128]{1,2,0:T(8,128)(2,1)}) %reduce-scatter.3.cloned.1.call-update) | async-done | bytes 262160 | tf_op jit(solution)/shard_map/reduce_scatter | solution.py:22
  221.2 0.0 reduce-scatter.5.cloned.1.call-update
  221.2 0.0 all-gather.5.cloned.1.call-start
  221.2 0.1 copy.33
  221.4 0.1 copy.36
  221.5 0.1 copy.38
  221.7 18.0 %reduce-scatter.5.cloned.1.call-done = bf16[1,512,128]{1,2,0:T(8,128)(2,1)} async-done(((bf16[2,512,128]{1,2,0:T(8,128)(2,1)}), bf16[1,512,128]{1,2,0:T(8,128)(2,1)}) %reduce-scatter.5.cloned.1.call-update) | async-done | bytes 131088 | tf_op jit(solution)/shard_map/reduce_scatter | solution.py:22
  239.7 1.8 fusion.14
  241.5 0.0 all-gather.5.cloned.1.call-update
  241.5 1.0 copy.39
  242.5 1.7 broadcast_in_dim.78
  244.3 7.5 %all-to-all-start.1 = ((bf16[16,512,128]{2,1,0:T(8,128)(2,1)}), bf16[16,512,128]{2,1,0:T(8,128)(2,1)S(1)}, u32[]{:S(2)}, u32[]{:S(2)}) async-start(bf16[16,512,128]{2,1,0:T(8,128)(2,1)} %broadcast_in_dim.78), calls=%async_computation.3 | async-start | bytes 4194304 | tf_op jit(solution)/shard_map/all_to_all | solution.py:38
  251.8 0.1 fusion.2
  251.9 0.1 iota_compare_fusion
  252.0 52.9 %all-gather.5.cloned.1.call-done = bf16[512,2048]{0,1:T(8,128)(2,1)} async-done(((bf16[512,128]{0,1:T(8,128)(2,1)}), bf16[512,2048]{0,1:T(8,128)(2,1)}) %all-gather.5.cloned.1.call-update) | async-done | bytes 2097168 | tf_op jit(solution)/shard_map/all_gather | solution.py:95
  304.9 19.3 %gather_fusion.1 = bf16[4096,512]{1,0:T(8,128)(2,1)} fusion(bf16[512,2048]{0,1:T(8,128)(2,1)} %all-gather.5.cloned.1.call-done, s32[4096]{0:T(1024)S(1)} %broadcast_clamp_fusion), kind=kCustom, calls=%fused_computation.1 | custom fusion | bytes 8404992 | tf_op jit(solution)/shard_map/jit(_take)/gather | solution.py:101
  324.2 5.2 %select_select_fusion = bf16[512,16,256]{0,2,1:T(8,128)(2,1)} fusion(bf16[512,16,256]{0,2,1:T(8,128)(2,1)} %bitcast.43, pred[16,256]{1,0:T(8,128)(4,1)S(1)} %get-tuple-element.30, pred[16,256]{1,0:T(8,128)(4,1)S(1)} %get-tuple-element.29), kind=kLoop, calls=%fused_computation.3 | loop fusion | flops 4194304 | bytes 8396800 | tf_op jit(solution)/shard_map/jit(_where)/select_n | solution.py:102
  329.5 0.0 all-to-all-done.1
  329.5 11.3 %all-to-all-start.2 = ((bf16[512,16,256]{0,2,1:T(8,128)(2,1)}), bf16[512,16,256]{0,2,1:T(8,128)(2,1)}, u32[]{:S(2)}, u32[]{:S(2)}) async-start(bf16[512,16,256]{0,2,1:T(8,128)(2,1)} %select_select_fusion), calls=%async_computation.4 | async-start | bytes 8388608 | tf_op jit(solution)/shard_map/all_to_all | solution.py:104
  340.7 0.8 copy.41
  341.6 0.8 copy.42
  342.4 0.8 copy.43
  343.2 93.3 %all-to-all-done.2 = bf16[512,16,256]{0,2,1:T(8,128)(2,1)} async-done(((bf16[512,16,256]{0,2,1:T(8,128)(2,1)}), bf16[512,16,256]{0,2,1:T(8,128)(2,1)}, u32[]{:S(2)}, u32[]{:S(2)}) %all-to-all-start.2) | async-done | bytes 4194336 | tf_op jit(solution)/shard_map/all_to_all | solution.py:104
  436.6 6.4 %copy.40 = bf16[16,512,1,256]{3,1,0,2:T(8,128)(2,1)} copy(bf16[16,512,1,256]{1,3,0,2:T(8,128)(2,1)} %bitcast.15) | data formatting | bytes 8388608 | tf_op jit(solution)/shard_map/all_to_all | solution.py:104
  443.0 1.3 copy.47
  (8 shorter events, 0.1 us)
Async XLA Ops:
  7.2 161.4 %all-gather.3.cloned.1.call-start = ((), (), s32[]{:S(2)}) async-start(), calls=%async_computation.5 | async-start | bytes 17825792 | tf_op jit(solution)/shard_map/all_gather | solution.py:86
  7.9 213.3 %reduce-scatter.3.cloned.1.call-start = ((), (), s32[]{:S(2)}) async-start(), calls=%async_computation.6 | async-start | bytes 2359296 | tf_op jit(solution)/shard_map/reduce_scatter | solution.py:22
  177.6 43.7 %copy-start = (f32[512,128]{1,0:T(8,128)S(1)}, f32[512,128]{1,0:T(8,128)}, u32[]{:S(2)}) copy-start(f32[512,128]{1,0:T(8,128)} %param.10) | copy-start | bytes 786436
  177.6 43.8 %copy-start.1 = (f32[512,128]{1,0:T(8,128)S(1)}, f32[512,128]{1,0:T(8,128)}, u32[]{:S(2)}) copy-start(f32[512,128]{1,0:T(8,128)} %param.11) | copy-start | bytes 786436
  177.6 43.9 %copy-start.2 = (f32[512,128]{1,0:T(8,128)S(1)}, f32[512,128]{1,0:T(8,128)}, u32[]{:S(2)}) copy-start(f32[512,128]{1,0:T(8,128)} %param.9) | copy-start | bytes 786436
  180.1 59.6 %reduce-scatter.5.cloned.1.call-start = ((), (), s32[]{:S(2)}) async-start(), calls=%async_computation.7 | async-start | bytes 393216 | tf_op jit(solution)/shard_map/reduce_scatter | solution.py:22
  221.2 83.7 %all-gather.5.cloned.1.call-start = ((), (), s32[]{:S(2)}) async-start(), calls=%async_computation.8 | async-start | bytes 2228224 | tf_op jit(solution)/shard_map/all_gather | solution.py:95
  244.3 85.2 %all-to-all-start.1 = ((bf16[16,512,128]{2,1,0:T(8,128)(2,1)}), bf16[16,512,128]{2,1,0:T(8,128)(2,1)S(1)}, u32[]{:S(2)}, u32[]{:S(2)}) async-start(bf16[16,512,128]{2,1,0:T(8,128)(2,1)} %broadcast_in_dim.78), calls=%async_computation.3 | async-start | bytes 4194304 | tf_op jit(solution)/shard_map/all_to_all | solution.py:38
  329.5 107.1 %all-to-all-start.2 = ((bf16[512,16,256]{0,2,1:T(8,128)(2,1)}), bf16[512,16,256]{0,2,1:T(8,128)(2,1)}, u32[]{:S(2)}, u32[]{:S(2)}) async-start(bf16[512,16,256]{0,2,1:T(8,128)(2,1)} %select_select_fusion), calls=%async_computation.4 | async-start | bytes 8388608 | tf_op jit(solution)/shard_map/all_to_all | solution.py:104
Sparse Core Ops, SparseCore 0:
  10.5 158.0 all-gather.2
  180.3 40.8 reduce-scatter.2
  223.7 16.0 reduce-scatter.4
  242.8 62.0 all-gather.4
where the time goes:
time: 452 us; the launch traced here: 451 us
  waiting for transfers between devices  270 us (60%)
  blocking collectives  73.9 us (16%)
  local copies, waits for them, and re-layouts  46.9 us (10%)
  other arithmetic  19.1 us (4%)
  starting transfers between devices  18.9 us (4%)
  between operations  13.9 us (3%)
  matrix products  8.12 us (2%)
    all_to_all x1, waiting for transfers between devices, on_device(): lax.all_to_all(outgoing, REP, split_axis=1, concat_axis=0, tiled=True)  93.3 us
    all_to_all x1, blocking collectives, on_device(): lax.all_to_all(spread, 'tp', split_axis=1, concat_axis=1, tiled=True)  73.9 us
    all_gather x1, waiting for transfers between devices, on_device(): lax.all_gather(tokens, 'tp', axis=1, tiled=True)  63.9 us
    reduce_scatter x2, waiting for transfers between devices, own_block(): parts = lax.psum_scatter(parts, axes[k], scatter_dimension=0, tiled=True)  59 us
    all_gather x1, waiting for transfers between devices, on_device(): replica_rows = lax.all_gather(weights, 'tp', axis=1, tiled=True)  52.9 us
    gather x1, local copies, waits for them, and re-layouts, on_device(): jnp.take(replica_rows, jnp.clip(source_cols, 0, COLS - 1).reshape(-1), ax...  19.3 us
    all_to_all x1, starting transfers between devices, on_device(): lax.all_to_all(outgoing, REP, split_axis=1, concat_axis=0, tiled=True)  11.3 us
    gather x1, local copies, waits for them, and re-layouts, on_device(): picked = jnp.take(grad_out, jnp.clip(offset, 0, slot_width - 1), axis=1)  9.61 us
  transfers between devices with their start and end apart: 6, of which 5 were waited for; matrix products, arithmetic and copies ran while one was open for 12% of the time, Pallas kernels for 0%

commit v1 on v0

--- a/solution.py
+++ b/solution.py
@@ -101,7 +101,10 @@
     taken = jnp.take(replica_rows, jnp.clip(source_cols, 0, COLS - 1).reshape(-1), axis=1)
     outgoing = jnp.where(valid.reshape(-1)[None, :], taken, jnp.zeros_like(taken))
     outgoing = outgoing.reshape(replica_rows.shape[0], replicas, slot_width)
-    arrived = lax.all_to_all(outgoing, REP, split_axis=1, concat_axis=0, tiled=True)
+    arrived = jnp.concatenate(
+        lax.all_to_all(jnp.stack(jnp.split(outgoing, lax.axis_size(REP), axis=1)), REP, 0, 0),
+        axis=0,
+    )
     slot_weights = arrived.reshape(1, -1, slot_width)
     return (new_master, new_first, new_second, healthy, slot_weights)
 

time: 452 us -> 462 us (1.022)
  local copies, waits for them, and re-layouts: 46.9 us -> 58.4 us
    unnamed x16 -> x31, local copies, waits for them, and re-layouts: 6.35 us -> 17.1 us
  transfers between devices with their start and end apart: 6 -> 6, of which waited for: 5 -> 5; matrix products, arithmetic and copies ran while one was open for 12% -> 14% of each run, Pallas kernels for 0% -> 0%
where the time goes in v1:
time: 462 us; the launch traced here: 461 us
  waiting for transfers between devices  270 us (58%)
  blocking collectives  73.9 us (16%)
  local copies, waits for them, and re-layouts  58.4 us (13%)
  starting transfers between devices  18.9 us (4%)
  other arithmetic  17.5 us (4%)
  between operations  14 us (3%)
  matrix products  8.12 us (2%)
    all_to_all x1, waiting for transfers between devices, on_device(): lax.all_to_all(jnp.stack(jnp.split(outgoing, lax.axis_size(REP), axis=1))...  93.3 us
    all_to_all x1, blocking collectives, on_device(): lax.all_to_all(spread, 'tp', split_axis=1, concat_axis=1, tiled=True)  73.9 us
    all_gather x1, waiting for transfers between devices, on_device(): lax.all_gather(tokens, 'tp', axis=1, tiled=True)  63.9 us
    reduce_scatter x2, waiting for transfers between devices, own_block(): parts = lax.psum_scatter(parts, axes[k], scatter_dimension=0, tiled=True)  59 us
    all_gather x1, waiting for transfers between devices, on_device(): replica_rows = lax.all_gather(weights, 'tp', axis=1, tiled=True)  53.1 us
    gather x1, local copies, waits for them, and re-layouts, on_device(): jnp.take(replica_rows, jnp.clip(source_cols, 0, COLS - 1).reshape(-1), ax...  19.3 us
    unnamed x31, local copies, waits for them, and re-layouts  17.1 us
    all_to_all x1, starting transfers between devices, on_device(): lax.all_to_all(jnp.stack(jnp.split(outgoing, lax.axis_size(REP), axis=1))...  11.3 us
  transfers between devices with their start and end apart: 6, of which 5 were waited for; matrix products, arithmetic and copies ran while one was open for 14% of the time, Pallas kernels for 0%

profile of v1, /device:TPU:32, one launch (start us, length us, event | category | flops | bytes accessed | tf_op | source)
XLA Modules:
  0.0 460.9 jit_solution(7702166508178307617)
XLA Ops:
  7.2 0.7 all-gather.3.cloned.1.call-update
  8.0 0.9 reduce_window_sum.11
  8.8 1.2 copy.34
  10.1 0.8 select_reduce_fusion.1
  10.9 1.3 fusion.28
  12.2 0.7 compare_select_fusion.1
  12.9 9.6 %gather_fusion = bf16[2048,1024]{1,0:T(8,128)(2,1)} fusion(bf16[1024,256]{0,1:T(8,128)(2,1)S(1)} %copy.34, s32[2048]{0:T(1024)S(1)} %broadcast_clamp_fusion.1), kind=kCustom, calls=%fused_computation | custom fusion | bytes 8396800 | tf_op jit(solution)/shard_map/jit(_take)/gather | solution.py:79
  22.5 0.7 fusion.26
  23.2 1.3 fusion.27
  24.5 3.1 select_select_fusion.1
  27.6 73.9 %all_to_all.15 = bf16[1024,16,128]{0,2,1:T(8,128)(2,1)} all-to-all(bf16[1024,16,128]{0,2,1:T(8,128)(2,1)S(1)} %select_select_fusion.1), channel_id=1, replica_groups=mesh['rep_0'=2,'rep_1'=8,'tp'=16] {'tp'}, dimensions={1} | all-to-all | bytes 8388608 | tf_op jit(solution)/shard_map/all_to_all | solution.py:83
  101.5 3.1 reduce_sum.50
  104.7 63.9 %all-gather.3.cloned.1.call-done = bf16[1024,8192]{1,0:T(8,128)(2,1)} async-done(((bf16[1024,512]{1,0:T(8,128)(2,1)}), bf16[1024,8192]{1,0:T(8,128)(2,1)}) %all-gather.3.cloned.1.call-update) | async-done | bytes 16777232 | tf_op jit(solution)/shard_map/all_gather | solution.py:86
  168.6 8.1 %convolution_convert_fusion = bf16[128,8192]{1,0:T(8,128)(2,1)S(1)} fusion(bf16[1024,128]{0,1:T(8,128)(2,1)S(1)} %reduce_sum.50, bf16[1024,8192]{1,0:T(8,128)(2,1)} %all-gather.3.cloned.1.call-done), kind=kOutput, calls=%fused_computation.2 | convolution fusion | flops 2148532224 | bytes 19136512 | tf_op jit(solution)/shard_map/dot_general | solution.py:85
  176.7 0.9 copy.44
  177.6 2.5 copy.35
  180.2 41.0 %reduce-scatter.3.cloned.1.call-done = bf16[2,512,128]{1,2,0:T(8,128)(2,1)} async-done(((bf16[16,512,128]{1,2,0:T(8,128)(2,1)}), bf16[2,512,128]{1,2,0:T(8,128)(2,1)}) %reduce-scatter.3.cloned.1.call-update) | async-done | bytes 262160 | tf_op jit(solution)/shard_map/reduce_scatter | solution.py:22
  221.7 18.0 %reduce-scatter.5.cloned.1.call-done = bf16[1,512,128]{1,2,0:T(8,128)(2,1)} async-done(((bf16[2,512,128]{1,2,0:T(8,128)(2,1)}), bf16[1,512,128]{1,2,0:T(8,128)(2,1)}) %reduce-scatter.5.cloned.1.call-update) | async-done | bytes 131088 | tf_op jit(solution)/shard_map/reduce_scatter | solution.py:22
  239.7 1.8 fusion.30
  241.7 1.0 copy.39
  242.8 1.7 broadcast_in_dim.78
  244.5 7.5 %all-to-all-start.1 = ((bf16[16,512,128]{2,1,0:T(8,128)(2,1)}), bf16[16,512,128]{2,1,0:T(8,128)(2,1)S(1)}, u32[]{:S(2)}, u32[]{:S(2)}) async-start(bf16[16,512,128]{2,1,0:T(8,128)(2,1)} %broadcast_in_dim.78), calls=%async_computation.3 | async-start | bytes 4194304 | tf_op jit(solution)/shard_map/all_to_all | solution.py:38
  252.0 53.1 %all-gather.5.cloned.1.call-done = bf16[512,2048]{0,1:T(8,128)(2,1)} async-done(((bf16[512,128]{0,1:T(8,128)(2,1)}), bf16[512,2048]{0,1:T(8,128)(2,1)}) %all-gather.5.cloned.1.call-update) | async-done | bytes 2097168 | tf_op jit(solution)/shard_map/all_gather | solution.py:95
  305.2 19.3 %gather_fusion.1 = bf16[4096,512]{1,0:T(8,128)(2,1)} fusion(bf16[512,2048]{0,1:T(8,128)(2,1)} %all-gather.5.cloned.1.call-done, s32[4096]{0:T(1024)S(1)} %broadcast_clamp_fusion), kind=kCustom, calls=%fused_computation.1 | custom fusion | bytes 8404992 | tf_op jit(solution)/shard_map/jit(_take)/gather | solution.py:101
  324.5 3.6 select_select_fusion
  328.1 0.7 fusion.17
  328.8 0.7 fusion.16
  329.5 0.7 fusion.15
  330.2 0.7 fusion.14
  331.0 0.7 fusion.13
  331.7 0.7 fusion.12
  332.4 0.7 fusion.11
  333.1 0.7 fusion.10
  333.8 0.7 fusion.9
  334.6 0.7 fusion.8
  335.3 0.7 fusion.7
  336.0 0.7 fusion.6
  336.7 0.7 fusion.5
  337.4 0.7 fusion.4
  338.2 0.7 fusion.3
  338.9 0.7 fusion.2
  339.6 11.3 %all-to-all-start.2 = ((bf16[16,512,1,256]{1,3,2,0:T(8,128)(2,1)}), bf16[16,512,1,256]{1,3,2,0:T(8,128)(2,1)}, u32[]{:S(2)}, u32[]{:S(2)}) async-start(bf16[16,512,1,256]{1,3,2,0:T(8,128)(2,1)} %fusion.2), calls=%async_computation.4 | async-start | bytes 8388608 | tf_op jit(solution)/shard_map/all_to_all | solution.py:105
  350.9 0.8 copy.41
  351.7 0.8 copy.42
  352.5 0.8 copy.43
  353.4 93.3 %all-to-all-done.2 = bf16[16,512,1,256]{1,3,2,0:T(8,128)(2,1)} async-done(((bf16[16,512,1,256]{1,3,2,0:T(8,128)(2,1)}), bf16[16,512,1,256]{1,3,2,0:T(8,128)(2,1)}, u32[]{:S(2)}, u32[]{:S(2)}) %all-to-all-start.2) | async-done | bytes 4194336 | tf_op jit(solution)/shard_map/all_to_all | solution.py:105
  446.7 6.4 %copy.40 = bf16[16,512,1,256]{3,1,0,2:T(8,128)(2,1)} copy(bf16[16,512,1,256]{1,3,2,0:T(8,128)(2,1)} %all-to-all-done.2) | data formatting | bytes 8388608 | tf_op jit(solution)/shard_map/all_to_all | solution.py:105
  453.1 1.3 copy.62
  (24 shorter events, 0.8 us)
Async XLA Ops:
  7.2 161.4 %all-gather.3.cloned.1.call-start = ((), (), s32[]{:S(2)}) async-start(), calls=%async_computation.5 | async-start | bytes 17825792 | tf_op jit(solution)/shard_map/all_gather | solution.py:86
  7.9 213.3 %reduce-scatter.3.cloned.1.call-start = ((), (), s32[]{:S(2)}) async-start(), calls=%async_computation.6 | async-start | bytes 2359296 | tf_op jit(solution)/shard_map/reduce_scatter | solution.py:22
  177.6 43.7 %copy-start = (f32[512,128]{1,0:T(8,128)S(1)}, f32[512,128]{1,0:T(8,128)}, u32[]{:S(2)}) copy-start(f32[512,128]{1,0:T(8,128)} %param.10) | copy-start | bytes 786436
  177.6 43.8 %copy-start.1 = (f32[512,128]{1,0:T(8,128)S(1)}, f32[512,128]{1,0:T(8,128)}, u32[]{:S(2)}) copy-start(f32[512,128]{1,0:T(8,128)} %param.11) | copy-start | bytes 786436
  177.6 43.9 %copy-start.2 = (f32[512,128]{1,0:T(8,128)S(1)}, f32[512,128]{1,0:T(8,128)}, u32[]{:S(2)}) copy-start(f32[512,128]{1,0:T(8,128)} %param.9) | copy-start | bytes 786436
  180.1 59.6 %reduce-scatter.5.cloned.1.call-start = ((), (), s32[]{:S(2)}) async-start(), calls=%async_computation.7 | async-start | bytes 393216 | tf_op jit(solution)/shard_map/reduce_scatter | solution.py:22
  221.2 84.0 %all-gather.5.cloned.1.call-start = ((), (), s32[]{:S(2)}) async-start(), calls=%async_computation.8 | async-start | bytes 2228224 | tf_op jit(solution)/shard_map/all_gather | solution.py:95
  244.5 95.1 %all-to-all-start.1 = ((bf16[16,512,128]{2,1,0:T(8,128)(2,1)}), bf16[16,512,128]{2,1,0:T(8,128)(2,1)S(1)}, u32[]{:S(2)}, u32[]{:S(2)}) async-start(bf16[16,512,128]{2,1,0:T(8,128)(2,1)} %broadcast_in_dim.78), calls=%async_computation.3 | async-start | bytes 4194304 | tf_op jit(solution)/shard_map/all_to_all | solution.py:38
  339.6 107.1 %all-to-all-start.2 = ((bf16[16,512,1,256]{1,3,2,0:T(8,128)(2,1)}), bf16[16,512,1,256]{1,3,2,0:T(8,128)(2,1)}, u32[]{:S(2)}, u32[]{:S(2)}) async-start(bf16[16,512,1,256]{1,3,2,0:T(8,128)(2,1)} %fusion.2), calls=%async_computation.4 | async-start | bytes 8388608 | tf_op jit(solution)/shard_map/all_to_all | solution.py:105
Sparse Core Ops, SparseCore 0:
  10.5 158.0 all-gather.2
  180.3 40.8 reduce-scatter.2
  223.7 16.0 reduce-scatter.4
  242.8 62.2 all-gather.4
